TPU v7x, 32 devices: a whole 2x2x4 slice. The times are simulated.
32 devices in a mesh: band: 4 (over y, x), dom: 8 (over z, core).
Axes of the slice: x: 2, y: 2, z: 4, core: 2. Of those that a mesh axis runs over, the one named last changes fastest.
Arguments:
- orbitals: float32 [1024, 32768], P('band', 'dom'), may hold values from -6 to 6
- projectors: float32 [256, 512, 128], P('dom'), may hold values from -0.25 to 0.25
- window_start: int32 [256], P('dom'), may hold values from 0 to 3584
- slot_atom: int32 [8, 32], replicated, may hold values from 0 to 23, as said below
- atom_home: int32 [24], replicated, may hold values from 0 to 23, as said below
- atom_matrices: float32 [24, 128, 128], P('dom'), may hold values from -0.1875 to 0.1875
- rotation: float32 [1024, 1024], P('band'), may hold values from -0.1875 to 0.1875
Outputs:
- rotated: float32 [1024, 32768], P('band', 'dom')
Inputs may be any that keep to these rules, and one draw needn't show every extreme that they name: `atom_home`: a permutation; atom a is owned by domain atom_home[a] // 3, so every domain owns 3 atoms. `slot_atom`: in one domain at most 8 windows have atoms of one owner; in every domain some owner has exactly 8 of them, and some owner has exactly 8 from every domain.
All inputs are finite; a program needn't handle non-finite values.
Results may differ from a plain program's by a relative error of at most 0.0003.
Values sent between devices are 32-bit elements; how exact they have to be, the bound alone decides.
No kernel may reach another device: no remote copies, remote signals or barrier semaphores. Data moves between devices by JAX's collectives and lax.ppermute only.
A program may use at most 128 MiB of HBM per device.

v0:
```python
import jax
import jax.numpy as jnp
from jax import lax
from jax.sharding import PartitionSpec as P

HIGHEST = lax.Precision.HIGHEST


def per_device(orbitals, projectors, window_start, slot_atom, atom_home, atom_matrices, rotation):
    own_domain = lax.axis_index("dom")
    slot_count = projectors.shape[0]
    window = projectors.shape[1]
    atom_count = atom_home.shape[0]
    columns = rotation
    base_field = jnp.dot(
        columns,
        lax.all_gather(orbitals, "band", axis=0, tiled=True),
        precision=HIGHEST,
        preferred_element_type=jnp.float32,
    )
    windows = jax.vmap(lambda offset: lax.dynamic_slice_in_dim(orbitals, offset, window, 1))(
        window_start
    )
    partials = jnp.einsum("sbw,swp->sbp", windows, projectors, precision=HIGHEST)
    atom_ids = jnp.arange(atom_count, dtype=jnp.int32)
    home_table = jnp.sum(
        jnp.where(slot_atom[:, :, None] == atom_ids[None, None, :], atom_home[None, None, :], 0),
        axis=2,
    )
    own_home = lax.dynamic_index_in_dim(home_table, own_domain, 0, keepdims=False)
    home_match = (atom_ids[:, None] == own_home[None, :]).astype(jnp.float32)
    per_atom = jnp.einsum("rs,sbp->rbp", home_match, partials, precision=HIGHEST)
    owned_sums = lax.psum_scatter(per_atom, "dom", scatter_dimension=0, tiled=True)
    owned_factors = jnp.einsum("abp,apq->abq", owned_sums, atom_matrices, precision=HIGHEST)
    columns = rotation
    owned_factors = jnp.einsum(
        "bc,scp->sbp",
        columns,
        lax.all_gather(owned_factors, "band", axis=1, tiled=True),
        precision=HIGHEST,
    )
    all_factors = lax.all_gather(owned_factors, "dom", axis=0, tiled=True)
    slot_factors = jnp.einsum("rs,rbp->sbp", home_match, all_factors, precision=HIGHEST)
    updates = jnp.einsum("sbq,swq->sbw", slot_factors, projectors, precision=HIGHEST)

    def add_window(slot_index, current):
        offset = window_start[slot_index]
        previous = lax.dynamic_slice_in_dim(current, offset, window, 1)
        return lax.dynamic_update_slice_in_dim(current, previous + updates[slot_index], offset, 1)

    corrected = lax.fori_loop(0, slot_count, add_window, base_field)
    return corrected


def solution(mesh):
    in_specs = (
        P("band", "dom"),
        P("dom", None, None),
        P("dom"),
        P(),
        P(),
        P("dom", None, None),
        P("band", None),
    )
    out_specs = P("band", "dom")
    return jax.shard_map(
        per_device, mesh=mesh, in_specs=in_specs, out_specs=out_specs, check_vma=False
    )
```

profile of v0, /device:TPU:0, one launch (start us, length us, event | category | flops | bytes accessed | tf_op | source)
XLA Modules:
  0.0 689.3 jit_solution(3986818245490201017)
XLA Ops:
  7.3 107.7 %while.15 = (s32[]{:T(128)}, f32[256,4096]{1,0:T(8,128)}, s32[32,2]{0,1:T(2,128)S(1)}, f32[32,256,512]{2,1,0:T(8,128)}, s32[]{:T(128)}) while((s32[]{:T(128)}, f32[256,4096]{1,0:T(8,128)}, s32[32,2]{0,1:T(2,128)S(1)}, f32[32,256,512]{2,1,0:T(8,128)}, s32[]{:T(128)}) %tuple.39), condition=%wide.while_cond, body=%wide.while_body.sunk | while | flops 2 | bytes 1049689 | solution.py:21
  115.1 19.3 %fusion.14 = f32[32,256,128]{2,1,0:T(8,128)S(1)} fusion(f32[32,256,512]{2,1,0:T(8,128)} %get-tuple-element.92, f32[32,512,128]{2,1,0:T(8,128)} %param.10), kind=kOutput, calls=%fused_computation.21 | convolution fusion | flops 6442450944 | bytes 29360128 | tf_op jit(solution)/shard_map/sbw,swp->sbp/dot_general | solution.py:24
  134.4 4.3 fusion.2
  141.0 43.3 %reduce-scatter.2.cloned.1.call-done = f32[3,256,128]{2,1,0:T(8,128)} async-done(((f32[24,256,128]{2,1,0:T(8,128)}), f32[3,256,128]{2,1,0:T(8,128)}) %reduce-scatter.2.cloned.1.call-update) | async-done | bytes 393232 | tf_op jit(solution)/shard_map/reduce_scatter | solution.py:33
  186.7 30.0 %all-gather.6.cloned.1.call-done = f32[3,1024,128]{2,1,0:T(8,128)} async-done(((f32[3,256,128]{2,1,0:T(8,128)}), f32[3,1024,128]{2,1,0:T(8,128)}) %all-gather.6.cloned.1.call-update) | async-done | bytes 1572880 | tf_op jit(solution)/shard_map/all_gather | solution.py:39
  216.7 4.0 convolution_bitcast_fusion
  222.3 37.8 %all-gather.8.cloned.1.call-done = f32[24,256,128]{2,1,0:T(8,128)} async-done(((f32[3,256,128]{2,1,0:T(8,128)}), f32[24,256,128]{2,1,0:T(8,128)}) %all-gather.8.cloned.1.call-update) | async-done | bytes 3145744 | tf_op jit(solution)/shard_map/all_gather | solution.py:42
  260.1 5.8 fusion.4
  265.9 21.7 %fusion = f32[32,256,512]{2,1,0:T(8,128)} fusion(f32[32,512,128]{2,1,0:T(8,128)} %param.10, f32[32,256,128]{2,0,1:T(8,128)S(1)} %fusion.4), kind=kOutput, calls=%fused_computation.3 | convolution fusion | flops 6442450944 | bytes 29360128 | tf_op jit(solution)/shard_map/sbq,swq->sbw/dot_general | solution.py:44
  287.6 130.4 %all-gather.4.cloned.1.call-done = f32[1024,4096]{1,0:T(8,128)} async-done(((f32[256,4096]{1,0:T(8,128)}), f32[1024,4096]{1,0:T(8,128)}) %all-gather.4.cloned.1.call-update) | async-done | bytes 16777232 | tf_op jit(solution)/shard_map/all_gather | solution.py:17
  418.0 18.0 %fusion.13 = f32[256,4096]{1,0:T(8,128)} fusion(f32[256,1024]{1,0:T(8,128)S(1)} %copy-done, f32[1024,4096]{1,0:T(8,128)} %all-gather.4.cloned.1.call-done), kind=kOutput, calls=%fused_computation.20 | convolution fusion | flops 12884901888 | bytes 22020096 | tf_op jit(solution)/shard_map/dot_general | solution.py:15
  436.0 246.8 %while.14 = (s32[]{:T(128)}, f32[256,4096]{1,0:T(8,128)}, s32[32]{0:T(128)S(1)}, f32[32,256,512]{2,1,0:T(8,128)}, s32[]{:T(128)}, /*index=5*/s32[]{:T(128)}, s32[]{:T(128)}) while((s32[]{:T(128)}, f32[256,4096]{1,0:T(8,128)}, s32[32]{0:T(128)S(1)}, f32[32,256,512]{2,1,0:T(8,128)}, s32[]{:T(128)}, /*index=5*/s32[]{:T(128)}, s32[]{:T(128)}) %tuple.53), condition=%wide.region_3.4_spmd, body=%wide.region_2.3_spmd.sunk | while | flops 131077 | bytes 2621575 | solution.py:51
  439.9 3.8 dynamic_update_slice.8
  447.6 3.8 dynamic_update_slice.8
  455.4 3.8 dynamic_update_slice.8
  463.1 3.8 dynamic_update_slice.8
  470.8 3.8 dynamic_update_slice.8
  478.5 3.8 dynamic_update_slice.8
  486.2 3.8 dynamic_update_slice.8
  509.2 3.8 dynamic_update_slice.8
  540.1 3.8 dynamic_update_slice.8
  547.8 3.8 dynamic_update_slice.8
  609.5 3.8 dynamic_update_slice.8
  617.2 3.8 dynamic_update_slice.8
  (206 shorter events, 256.6 us)
Async XLA Ops:
  6.5 210.2 %copy-start = (f32[256,1024]{1,0:T(8,128)S(1)}, f32[256,1024]{1,0:T(8,128)}, u32[]{:S(2)}) copy-start(f32[256,1024]{1,0:T(8,128)} %param.15) | copy-start | bytes 3145732
  6.5 108.5 %copy-start.2 = (s32[8,32]{1,0:T(8,128)S(1)}, s32[8,32]{1,0:T(8,128)}, u32[]{:S(2)}) copy-start(s32[8,32]{1,0:T(8,128)} %param.12) | copy-start | bytes 3076
  6.5 108.5 %copy-start.3 = (s32[24]{0:T(128)S(1)}, s32[24]{0:T(128)}, u32[]{:S(2)}) copy-start(s32[24]{0:T(128)} %param.13) | copy-start | bytes 292
  6.5 177.7 %reduce-scatter.2.cloned.1.call-start = ((), (), s32[]{:S(2)}) async-start(), calls=%async_computation.2 | async-start | bytes 3538944 | tf_op jit(solution)/shard_map/reduce_scatter | solution.py:33
  138.7 45.6 %copy-start.1 = (f32[3,128,128]{2,1,0:T(8,128)S(1)}, f32[3,128,128]{2,1,0:T(8,128)}, u32[]{:S(2)}) copy-start(f32[3,128,128]{2,1,0:T(8,128)} %param.14) | copy-start | bytes 589828
  140.9 75.8 %all-gather.6.cloned.1.call-start = ((), (), s32[]{:S(2)}) async-start(), calls=%async_computation.3 | async-start | bytes 1966080 | tf_op jit(solution)/shard_map/all_gather | solution.py:39
  186.5 73.6 %all-gather.8.cloned.1.call-start = ((), (), s32[]{:S(2)}) async-start(), calls=%async_computation.4 | async-start | bytes 3538944 | tf_op jit(solution)/shard_map/all_gather | solution.py:42
  221.7 196.3 %all-gather.4.cloned.1.call-start = ((), (), s32[]{:S(2)}) async-start(), calls=%async_computation.1 | async-start | bytes 20971520 | tf_op jit(solution)/shard_map/all_gather | solution.py:17
  287.6 148.4 %copy-start.4 = (s32[32]{0:T(128)S(1)}, s32[32]{0:T(128)}, u32[]{:S(2)}) copy-start(s32[32]{0:T(128)} %param.11) | copy-start | bytes 388
Sparse Core Ops, SparseCore 0:
  141.1 43.1 reduce-scatter.1
  186.6 30.0 all-gather.5
  221.8 38.2 all-gather.7
  261.8 156.1 all-gather.3
where the time goes:
time: 695 us; the launch traced here: 689 us
  local copies, waits for them, and re-layouts  251 us (36%)
  waiting for transfers between devices  242 us (35%)
  matrix products  75.2 us (11%)
  loops' own time  59.9 us (9%)
  other arithmetic  47.5 us (7%)
  between operations  13.2 us (2%)
    all_gather x1, waiting for transfers between devices, per_device(): lax.all_gather(orbitals, 'band', axis=0, tiled=True)  130 us
    dynamic_update_slice x32, local copies, waits for them, and re-layouts, add_window(): lax.dynamic_update_slice_in_dim(current, previous + updates[slot_index],...  120 us
    gather x96, local copies, waits for them, and re-layouts  108 us
    another operation x1, loops' own time, per_device(): corrected = lax.fori_loop(0, slot_count, add_window, base_field)  59.9 us
    add x32, other arithmetic, add_window(): previous + updates[slot_index]  46.6 us
    reduce_scatter x1, waiting for transfers between devices, per_device(): lax.psum_scatter(per_atom, 'dom', scatter_dimension=0, tiled=True)  43.3 us
    all_gather x1, waiting for transfers between devices, per_device(): all_factors = lax.all_gather(owned_factors, 'dom', axis=0, tiled=True)  37.8 us
    all_gather x1, waiting for transfers between devices, per_device(): lax.all_gather(owned_factors, 'band', axis=1, tiled=True)  30 us
  transfers between devices with their start and end apart: 4, of which 4 were waited for; matrix products, arithmetic and copies ran while one was open for 4% of the time, Pallas kernels for 0%

commit v1 on v0

--- a/solution.py
+++ b/solution.py
@@ -39,7 +39,12 @@
         lax.all_gather(owned_factors, "band", axis=1, tiled=True),
         precision=HIGHEST,
     )
-    all_factors = lax.all_gather(owned_factors, "dom", axis=0, tiled=True)
+    ring = [owned_factors]
+    for hop in range(7):
+        ring.append(lax.ppermute(ring[-1], "dom", [(dev, (dev + 1) % 8) for dev in range(8)]))
+    all_factors = jnp.roll(
+        jnp.concatenate(ring[::-1], axis=0), (lax.axis_index("dom") + 1) * ring[0].shape[0], axis=0
+    )
     slot_factors = jnp.einsum("rs,rbp->sbp", home_match, all_factors, precision=HIGHEST)
     updates = jnp.einsum("sbq,swq->sbw", slot_factors, projectors, precision=HIGHEST)
 

time: 695 us -> 653 us (0.940)
  waiting for transfers between devices: 242 us -> 194 us
  local copies, waits for them, and re-layouts: 251 us -> 259 us
    all_gather x1, waiting for transfers between devices: 130 us -> 57.7 us  [per_device(): lax.all_gather(orbitals, 'band', axis=0, tiled=True)]
    ppermute x0 -> x7, waiting for transfers between devices: none -> 63.4 us  [per_device(): lax.ppermute(ring[-1], 'dom', [(dev, (dev + 1) % 8) for dev in range(8)])]
    all_gather x1 -> x0, waiting for transfers between devices: 37.8 us -> none  [per_device(): all_factors = lax.all_gather(owned_factors, 'dom', axis=0, tiled=True)]
  transfers between devices with their start and end apart: 4 -> 10, of which waited for: 4 -> 10; matrix products, arithmetic and copies ran while one was open for 4% -> 6% of each run, Pallas kernels for 0% -> 0%
where the time goes in v1:
time: 653 us; the launch traced here: 647 us
  local copies, waits for them, and re-layouts  259 us (40%)
  waiting for transfers between devices  194 us (30%)
  matrix products  71.2 us (11%)
  loops' own time  61.2 us (9%)
  other arithmetic  48.2 us (7%)
  between operations  13.3 us (2%)
    dynamic_update_slice x32, local copies, waits for them, and re-layouts, add_window(): lax.dynamic_update_slice_in_dim(current, previous + updates[slot_index],...  120 us
    gather x96, local copies, waits for them, and re-layouts  107 us
    ppermute x7, waiting for transfers between devices, per_device(): lax.ppermute(ring[-1], 'dom', [(dev, (dev + 1) % 8) for dev in range(8)])  63.4 us
    another operation x1, loops' own time, per_device(): corrected = lax.fori_loop(0, slot_count, add_window, base_field)  61.2 us
    all_gather x1, waiting for transfers between devices, per_device(): lax.all_gather(orbitals, 'band', axis=0, tiled=True)  57.7 us
    add x32, other arithmetic, add_window(): previous + updates[slot_index]  46.6 us
    reduce_scatter x1, waiting for transfers between devices, per_device(): lax.psum_scatter(per_atom, 'dom', scatter_dimension=0, tiled=True)  43.3 us
    all_gather x1, waiting for transfers between devices, per_device(): lax.all_gather(owned_factors, 'band', axis=1, tiled=True)  29.4 us
  transfers between devices with their start and end apart: 10, of which 10 were waited for; matrix products, arithmetic and copies ran while one was open for 6% of the time, Pallas kernels for 0%

profile of v1, /device:TPU:0, one launch (start us, length us, event | category | flops | bytes accessed | tf_op | source)
XLA Modules:
  0.0 647.4 jit_solution(543942780862168432)
XLA Ops:
  7.3 107.1 %while.15 = (s32[]{:T(128)}, f32[256,4096]{1,0:T(8,128)}, s32[32,2]{0,1:T(2,128)S(1)}, f32[32,256,512]{2,1,0:T(8,128)}, s32[]{:T(128)}) while((s32[]{:T(128)}, f32[256,4096]{1,0:T(8,128)}, s32[32,2]{0,1:T(2,128)S(1)}, f32[32,256,512]{2,1,0:T(8,128)}, s32[]{:T(128)}) %tuple.39), condition=%wide.while_cond, body=%wide.while_body.sunk | while | flops 2 | bytes 1049689 | solution.py:21
  115.2 19.3 %fusion.13 = f32[32,256,128]{2,1,0:T(8,128)S(1)} fusion(f32[32,256,512]{2,1,0:T(8,128)} %get-tuple-element.92, f32[32,512,128]{2,1,0:T(8,128)} %param.10), kind=kOutput, calls=%fused_computation.37 | convolution fusion | flops 6442450944 | bytes 29360128 | tf_op jit(solution)/shard_map/sbw,swp->sbp/dot_general | solution.py:24
  134.5 4.3 fusion.2
  141.1 43.3 %reduce-scatter.2.cloned.1.call-done = f32[3,256,128]{2,1,0:T(8,128)} async-done(((f32[24,256,128]{2,1,0:T(8,128)}), f32[3,256,128]{2,1,0:T(8,128)}) %reduce-scatter.2.cloned.1.call-update) | async-done | bytes 393232 | tf_op jit(solution)/shard_map/reduce_scatter | solution.py:33
  187.4 29.4 %all-gather.5.cloned.1.call-done = f32[3,1024,128]{1,2,0:T(8,128)} async-done(((f32[3,256,128]{1,2,0:T(8,128)}), f32[3,1024,128]{1,2,0:T(8,128)}) %all-gather.5.cloned.1.call-update) | async-done | bytes 1572880 | tf_op jit(solution)/shard_map/all_gather | solution.py:39
  219.7 9.0 %collective-permute-done = f32[3,256,128]{1,2,0:T(8,128)S(1)} collective-permute-done((f32[3,256,128]{1,2,0:T(8,128)S(1)}, f32[3,256,128]{1,2,0:T(8,128)S(1)}, u32[]{:S(2)}, u32[]{:S(2)}) %collective-permute-start) | collective-permute-done | bytes 393248 | tf_op jit(solution)/shard_map/ppermute | solution.py:44
  228.6 9.0 %collective-permute-done.1 = f32[3,256,128]{1,2,0:T(8,128)S(1)} collective-permute-done((f32[3,256,128]{1,2,0:T(8,128)S(1)}, f32[3,256,128]{1,2,0:T(8,128)S(1)}, u32[]{:S(2)}, u32[]{:S(2)}) %collective-permute-start.1) | collective-permute-done | bytes 393248 | tf_op jit(solution)/shard_map/ppermute | solution.py:44
  237.6 9.0 %collective-permute-done.2 = f32[3,256,128]{1,2,0:T(8,128)S(1)} collective-permute-done((f32[3,256,128]{1,2,0:T(8,128)S(1)}, f32[3,256,128]{1,2,0:T(8,128)S(1)}, u32[]{:S(2)}, u32[]{:S(2)}) %collective-permute-start.2) | collective-permute-done | bytes 393248 | tf_op jit(solution)/shard_map/ppermute | solution.py:44
  246.6 9.0 %collective-permute-done.3 = f32[3,256,128]{1,2,0:T(8,128)S(1)} collective-permute-done((f32[3,256,128]{1,2,0:T(8,128)S(1)}, f32[3,256,128]{1,2,0:T(8,128)S(1)}, u32[]{:S(2)}, u32[]{:S(2)}) %collective-permute-start.3) | collective-permute-done | bytes 393248 | tf_op jit(solution)/shard_map/ppermute | solution.py:44
  255.6 9.0 %collective-permute-done.4 = f32[3,256,128]{1,2,0:T(8,128)S(1)} collective-permute-done((f32[3,256,128]{1,2,0:T(8,128)S(1)}, f32[3,256,128]{1,2,0:T(8,128)S(1)}, u32[]{:S(2)}, u32[]{:S(2)}) %collective-permute-start.4) | collective-permute-done | bytes 393248 | tf_op jit(solution)/shard_map/ppermute | solution.py:44
  264.6 9.1 %collective-permute-done.5 = f32[3,256,128]{1,2,0:T(8,128)} collective-permute-done((f32[3,256,128]{1,2,0:T(8,128)S(1)}, f32[3,256,128]{1,2,0:T(8,128)}, u32[]{:S(2)}, u32[]{:S(2)}) %collective-permute-start.5) | collective-permute-done | bytes 393248 | tf_op jit(solution)/shard_map/ppermute | solution.py:44
  273.7 9.3 %collective-permute-done.6 = f32[3,256,128]{1,2,0:T(8,128)} collective-permute-done((f32[3,256,128]{1,2,0:T(8,128)}, f32[3,256,128]{1,2,0:T(8,128)}, u32[]{:S(2)}, u32[]{:S(2)}) %collective-permute-start.6) | collective-permute-done | bytes 393248 | tf_op jit(solution)/shard_map/ppermute | solution.py:44
  293.6 3.8 fusion.6
  297.4 20.8 %fusion = f32[32,256,512]{2,1,0:T(8,128)} fusion(f32[32,512,128]{2,1,0:T(8,128)} %param.10, f32[32,256,128]{2,0,1:T(8,128)S(1)} %fusion.6), kind=kOutput, calls=%fused_computation.3 | convolution fusion | flops 6442450944 | bytes 29360128 | tf_op jit(solution)/shard_map/sbq,swq->sbw/dot_general | solution.py:49
  318.2 57.7 %all-gather.3.cloned.1.call-done = f32[1024,4096]{1,0:T(8,128)} async-done(((f32[256,4096]{1,0:T(8,128)}), f32[1024,4096]{1,0:T(8,128)}) %all-gather.3.cloned.1.call-update) | async-done | bytes 16777232 | tf_op jit(solution)/shard_map/all_gather | solution.py:17
  375.9 18.0 %fusion.12 = f32[256,4096]{1,0:T(8,128)} fusion(f32[256,1024]{1,0:T(8,128)S(1)} %copy-done, f32[1024,4096]{1,0:T(8,128)} %all-gather.3.cloned.1.call-done), kind=kOutput, calls=%fused_computation.36 | convolution fusion | flops 12884901888 | bytes 22020096 | tf_op jit(solution)/shard_map/dot_general | solution.py:15
  393.9 247.0 %while.14 = (s32[]{:T(128)}, f32[256,4096]{1,0:T(8,128)}, s32[32]{0:T(128)S(1)}, f32[32,256,512]{2,1,0:T(8,128)}, s32[]{:T(128)}, /*index=5*/s32[]{:T(128)}, s32[]{:T(128)}) while((s32[]{:T(128)}, f32[256,4096]{1,0:T(8,128)}, s32[32]{0:T(128)S(1)}, f32[32,256,512]{2,1,0:T(8,128)}, s32[]{:T(128)}, /*index=5*/s32[]{:T(128)}, s32[]{:T(128)}) %tuple.51), condition=%wide.region_3.4_spmd, body=%wide.region_2.3_spmd.sunk | while | flops 131077 | bytes 2621575 | solution.py:56
  413.3 3.8 dynamic_update_slice.8
  428.7 3.8 dynamic_update_slice.8
  444.2 3.8 dynamic_update_slice.8
  498.1 3.8 dynamic_update_slice.8
  513.5 3.8 dynamic_update_slice.8
  529.0 3.8 dynamic_update_slice.8
  544.4 3.8 dynamic_update_slice.8
  (230 shorter events, 286.8 us)
Async XLA Ops:
  6.5 210.2 %copy-start = (f32[256,1024]{1,0:T(8,128)S(1)}, f32[256,1024]{1,0:T(8,128)}, u32[]{:S(2)}) copy-start(f32[256,1024]{1,0:T(8,128)} %param.15) | copy-start | bytes 3145732
  6.5 177.8 %reduce-scatter.2.cloned.1.call-start = ((), (), s32[]{:S(2)}) async-start(), calls=%async_computation.2 | async-start | bytes 3538944 | tf_op jit(solution)/shard_map/reduce_scatter | solution.py:33
  138.8 45.6 %copy-start.1 = (f32[3,128,128]{2,1,0:T(8,128)S(1)}, f32[3,128,128]{2,1,0:T(8,128)}, u32[]{:S(2)}) copy-start(f32[3,128,128]{2,1,0:T(8,128)} %param.14) | copy-start | bytes 589828
  141.0 75.7 %all-gather.5.cloned.1.call-start = ((), (), s32[]{:S(2)}) async-start(), calls=%async_computation.3 | async-start | bytes 1966080 | tf_op jit(solution)/shard_map/all_gather | solution.py:39
  186.6 189.3 %all-gather.3.cloned.1.call-start = ((), (), s32[]{:S(2)}) async-start(), calls=%async_computation.1 | async-start | bytes 20971520 | tf_op jit(solution)/shard_map/all_gather | solution.py:17
  219.6 9.1 %collective-permute-start = (f32[3,256,128]{1,2,0:T(8,128)S(1)}, f32[3,256,128]{1,2,0:T(8,128)S(1)}, u32[]{:S(2)}, u32[]{:S(2)}) collective-permute-start(f32[3,256,128]{1,2,0:T(8,128)S(1)} %convolution_bitcast_fusion), channel_id=1, source_target_pairs={{0,1},{1,2},{2,3},{3,4},{4,5},{5,6},{6,7},{7,0},{8,9},{9,10},{10,1... | collective-permute-start | bytes 1179656 | tf_op jit(solution)/shard_map/ppermute | solution.py:44
  228.6 9.0 %collective-permute-start.1 = (f32[3,256,128]{1,2,0:T(8,128)S(1)}, f32[3,256,128]{1,2,0:T(8,128)S(1)}, u32[]{:S(2)}, u32[]{:S(2)}) collective-permute-start(f32[3,256,128]{1,2,0:T(8,128)S(1)} %collective-permute-done), channel_id=1, source_target_pairs={{0,1},{1,2},{2,3},{3,4},{4,5},{5,6},{6,7},{7,0},{8,9},{9,10},{10,1... | collective-permute-start | bytes 1179656 | tf_op jit(solution)/shard_map/ppermute | solution.py:44
  237.6 9.0 %collective-permute-start.2 = (f32[3,256,128]{1,2,0:T(8,128)S(1)}, f32[3,256,128]{1,2,0:T(8,128)S(1)}, u32[]{:S(2)}, u32[]{:S(2)}) collective-permute-start(f32[3,256,128]{1,2,0:T(8,128)S(1)} %collective-permute-done.1), channel_id=1, source_target_pairs={{0,1},{1,2},{2,3},{3,4},{4,5},{5,6},{6,7},{7,0},{8,9},{9,10},{10,1... | collective-permute-start | bytes 1179656 | tf_op jit(solution)/shard_map/ppermute | solution.py:44
  246.6 9.0 %collective-permute-start.3 = (f32[3,256,128]{1,2,0:T(8,128)S(1)}, f32[3,256,128]{1,2,0:T(8,128)S(1)}, u32[]{:S(2)}, u32[]{:S(2)}) collective-permute-start(f32[3,256,128]{1,2,0:T(8,128)S(1)} %collective-permute-done.2), channel_id=1, source_target_pairs={{0,1},{1,2},{2,3},{3,4},{4,5},{5,6},{6,7},{7,0},{8,9},{9,10},{10,1... | collective-permute-start | bytes 1179656 | tf_op jit(solution)/shard_map/ppermute | solution.py:44
  255.6 9.0 %collective-permute-start.4 = (f32[3,256,128]{1,2,0:T(8,128)S(1)}, f32[3,256,128]{1,2,0:T(8,128)S(1)}, u32[]{:S(2)}, u32[]{:S(2)}) collective-permute-start(f32[3,256,128]{1,2,0:T(8,128)S(1)} %collective-permute-done.3), channel_id=1, source_target_pairs={{0,1},{1,2},{2,3},{3,4},{4,5},{5,6},{6,7},{7,0},{8,9},{9,10},{10,1... | collective-permute-start | bytes 1179656 | tf_op jit(solution)/shard_map/ppermute | solution.py:44
  264.6 9.1 %collective-permute-start.5 = (f32[3,256,128]{1,2,0:T(8,128)S(1)}, f32[3,256,128]{1,2,0:T(8,128)}, u32[]{:S(2)}, u32[]{:S(2)}) collective-permute-start(f32[3,256,128]{1,2,0:T(8,128)S(1)} %collective-permute-done.4), channel_id=1, source_target_pairs={{0,1},{1,2},{2,3},{3,4},{4,5},{5,6},{6,7},{7,0},{8,9},{9,10},{10,1... | collective-permute-start | bytes 1179656 | tf_op jit(solution)/shard_map/ppermute | solution.py:44
  273.7 9.3 %collective-permute-start.6 = (f32[3,256,128]{1,2,0:T(8,128)}, f32[3,256,128]{1,2,0:T(8,128)}, u32[]{:S(2)}, u32[]{:S(2)}) collective-permute-start(f32[3,256,128]{1,2,0:T(8,128)} %collective-permute-done.5), channel_id=1, source_target_pairs={{0,1},{1,2},{2,3},{3,4},{4,5},{5,6},{6,7},{7,0},{8,9},{9,10},{10,1... | collective-permute-start | bytes 1179656 | tf_op jit(solution)/shard_map/ppermute | solution.py:44
  318.2 75.7 %copy-start.2 = (s32[32]{0:T(128)S(1)}, s32[32]{0:T(128)}, u32[]{:S(2)}) copy-start(s32[32]{0:T(128)} %param.11) | copy-start | bytes 388
Sparse Core Ops, SparseCore 0:
  141.1 43.1 reduce-scatter.1
  186.8 29.9 all-gather.4
  218.6 157.2 all-gather.2
